TPU v7x, 32 devices: a whole 2x2x4 slice. The times are simulated.
32 devices in a mesh: ctx: 4 (over y, x), tp: 4 (over z), grp: 2 (over core).
Axes of the slice: x: 2, y: 2, z: 4, core: 2. Of those that a mesh axis runs over, the one named last changes fastest.
Arguments:
- patches: bfloat16 [32, 5120], P('ctx'), may hold values from -6 to 6
- route_count: int32 [4, 4], replicated, may hold values from 0 to 2, as said below
- text_states: bfloat16 [512, 4096], P('ctx', ('tp', 'grp')), may hold values from -6 to 6
- segment_ids: int32 [512], replicated, may hold values from 0 to 3, never falling along the last dimension, each value on 1 to 256 neighbouring positions
- vision_gain: float32 [1280], replicated, may hold values from 0.1 to 1.9
- merge_up: bfloat16 [5120, 2560], P(None, ('tp', 'grp')), may hold values from -0.078125 to 0.078125
- merge_down: bfloat16 [2560, 4096], P(('tp', 'grp')), may hold values from -0.125 to 0.125
- norm_gain: float32 [4096], replicated, may hold values from 0.1 to 1.9
- query_weight: bfloat16 [4096, 4096], P(None, ('tp', 'grp')), may hold values from -0.62928387 to 0.62928387
- kv_weight: bfloat16 [4096, 2048], P(None, 'tp'), may hold values from -0.4578688 to 0.4578688
Outputs:
- attended: bfloat16 [512, 4096], P('ctx', ('tp', 'grp'))
Inputs may be any that keep to these rules, and one draw needn't show every extreme that they name: route_count[c, d] counts the live rows among the 2 rows that source c holds for owner d; at least one owner gets 2 live rows from every source. `segment_ids`: never falling along the packed batch; a segment has at most 256 positions.
All inputs are finite; a program needn't handle non-finite values.
Results may differ from a plain program's by a relative error of at most 0.04.
Values may be sent and summed in bfloat16 or wider, within the bound.
A program may use at most 64 MiB of HBM per device.

v0:
```python
import jax
import jax.numpy as jnp
from jax import lax
from jax.sharding import PartitionSpec as P

HQ = 32
KVH = 8
HD = 128
EPSILON = 1e-06
NEGATIVE = -1e30


def rms_scale(values, gain):
    mean_square = jnp.mean(values * values, axis=-1, keepdims=True)
    return values * lax.rsqrt(mean_square + EPSILON) * gain


def attend(
    running,
    queries4,
    shard_piece,
    key_pos,
    query_pos,
    query_seg,
    segment_ids,
    visual_count,
    tokens_dev,
):
    weighted, running_max, denominator = running
    piece_rows = shard_piece.shape[0]
    kv_heads = queries4.shape[1]
    kv_split = shard_piece.reshape(piece_rows, kv_heads, 2, HD)
    key_block = kv_split[:, :, 0]
    value_block = kv_split[:, :, 1]
    key_owner = key_pos // tokens_dev
    owner_match = key_owner[:, None] == jnp.arange(visual_count.shape[0], dtype=jnp.int32)[None, :]
    visual_limit = jnp.sum(jnp.where(owner_match, visual_count[None, :], 0), axis=1)
    key_visual = key_pos % tokens_dev < visual_limit
    key_seg = segment_ids[key_pos]
    allowed = (query_seg[:, None] == key_seg[None, :]) & (
        key_visual[None, :] | (key_pos[None, :] <= query_pos[:, None])
    )
    scores = jnp.where(
        allowed,
        jnp.einsum("qkgd,rkd->kgqr", queries4, key_block, preferred_element_type=jnp.float32)
        * HD ** (-0.5),
        NEGATIVE,
    )
    new_max = jnp.maximum(running_max, jnp.max(scores, axis=-1))
    weights = jnp.exp(jnp.where(allowed, scores - new_max[..., None], NEGATIVE))
    denominator = jnp.sum(weights, axis=-1)
    weighted = jnp.einsum(
        "kgqr,rkd->kgqd",
        weights.astype(jnp.bfloat16),
        value_block,
        preferred_element_type=jnp.float32,
    )
    return (weighted, new_max, denominator)


def start_state(kv_heads, per_head, tokens_dev):
    return (
        jnp.zeros((kv_heads, per_head, tokens_dev, HD), jnp.float32),
        jnp.full((kv_heads, per_head, tokens_dev), NEGATIVE, jnp.float32),
        jnp.zeros((kv_heads, per_head, tokens_dev), jnp.float32),
    )


def shards(
    patches,
    route_count,
    text_states,
    segment_ids,
    vision_gain,
    merge_up,
    merge_down,
    norm_gain,
    query_weight,
    kv_weight,
):
    ctx_size = lax.axis_size("ctx")
    grp_size = lax.axis_size("grp")
    tp_size = lax.axis_size("tp")
    owner_index = lax.axis_index("ctx")
    member = lax.axis_index("grp")
    tp_index = lax.axis_index("tp")
    tensor_index = tp_index * grp_size + member
    row_count = patches.shape[0]
    bucket_rows = row_count // ctx_size
    tokens_dev = text_states.shape[0]
    grouped = patches.astype(jnp.float32).reshape(row_count, 4, -1)
    patch_normed = rms_scale(grouped, vision_gain).reshape(row_count, -1).astype(jnp.bfloat16)
    hidden = jax.nn.gelu(
        jnp.dot(patch_normed, merge_up, preferred_element_type=jnp.float32), approximate=False
    ).astype(jnp.bfloat16)
    partial_value = jnp.dot(hidden, merge_down, preferred_element_type=jnp.float32)
    column = lax.dynamic_slice_in_dim(route_count, owner_index, 1, 1)[:, 0]
    count_ends = jnp.cumsum(column)
    count_starts = count_ends - column
    slot_ids = jnp.arange(tokens_dev, dtype=jnp.int32)
    source = jnp.sum((count_ends[None, :] <= slot_ids[:, None]).astype(jnp.int32), axis=1)
    source = jnp.minimum(source, ctx_size - 1)
    source_match = source[:, None] == jnp.arange(ctx_size, dtype=jnp.int32)[None, :]
    first_slot = jnp.sum(jnp.where(source_match, count_starts[None, :], 0), axis=1)
    visual = slot_ids < count_ends[ctx_size - 1]
    pick_rows = jnp.where(visual, source * bucket_rows + slot_ids - first_slot, 0)
    merged = lax.psum(partial_value, ("tp", "grp")).astype(jnp.bfloat16)
    arrived = lax.all_to_all(
        merged.reshape(ctx_size, bucket_rows, -1), "ctx", split_axis=0, concat_axis=0, tiled=True
    )
    arrived = arrived.reshape(row_count, -1)
    text_full = lax.all_gather(text_states, ("tp", "grp"), axis=1, tiled=True)
    packed = jnp.where(visual[:, None], arrived[pick_rows], text_full)
    normal = rms_scale(packed.astype(jnp.float32), norm_gain).astype(jnp.bfloat16)
    queries = jnp.dot(normal, query_weight, preferred_element_type=jnp.float32).astype(jnp.bfloat16)
    kv_pairs = jnp.dot(normal, kv_weight, preferred_element_type=jnp.float32).astype(jnp.bfloat16)
    heads_dev = queries.shape[1] // HD
    group = HQ // KVH
    kv_per_tp = KVH // tp_size
    query_pos = owner_index * tokens_dev + slot_ids
    query_seg = segment_ids[query_pos]
    visual_count = jnp.sum(route_count, axis=0)
    kv_local = tensor_index * heads_dev // group - tp_index * kv_per_tp
    chosen = lax.dynamic_slice_in_dim(kv_pairs, kv_local * 2 * HD, 2 * HD, 1)
    queries4 = queries.reshape(tokens_dev, 1, heads_dev, HD)
    shard_piece = lax.all_gather(chosen, "ctx", axis=0, tiled=True)
    key_pos = jnp.arange(shard_piece.shape[0], dtype=jnp.int32)
    weighted, running_max, denominator = attend(
        start_state(1, heads_dev, tokens_dev),
        queries4,
        shard_piece,
        key_pos,
        query_pos,
        query_seg,
        segment_ids,
        visual_count,
        tokens_dev,
    )
    result = (weighted / denominator[..., None]).reshape(heads_dev, tokens_dev, HD)
    return result.transpose(1, 0, 2).reshape(tokens_dev, -1).astype(jnp.bfloat16)


def solution(mesh):
    return jax.shard_map(
        shards,
        mesh=mesh,
        in_specs=(
            P("ctx", None),
            P(),
            P("ctx", ("tp", "grp")),
            P(),
            P(),
            P(None, ("tp", "grp")),
            P(("tp", "grp"), None),
            P(),
            P(None, ("tp", "grp")),
            P(None, "tp"),
        ),
        out_specs=P("ctx", ("tp", "grp")),
        check_vma=False,
    )
```

profile of v0, /device:TPU:0, one launch (start us, length us, event | category | flops | bytes accessed | tf_op | source)
XLA Modules:
  0.0 106.3 jit_solution(12033060647353405200)
XLA Ops:
  6.5 0.0 copy-start
  6.5 1.0 convert_multiply_fusion.3
  7.6 0.1 reduce_sum.67
  7.7 0.7 mul.112
  8.4 0.1 mul.109
  8.5 0.0 copy-done
  8.5 0.0 copy-start.5
  8.5 0.0 copy-start.1
  8.5 4.6 %fusion.41 = f32[8,4096]{1,0:T(8,128)} fusion(bf16[320,4096]{1,0:T(8,128)(2,1)} %param.16, bf16[5120,320]{0,1:T(8,128)(2,1)S(1)} %copy-done, f32[8,5120]{1,0:T(8,128)S(1)} %bitcast.59, bf16[8,5120]{1,0:T(8,128)(2,1)} %param.10, f32[5120]{0:T(1024)S(1)} %mul.113), kind=kOutput, calls=%fused_computation.58 | convolution fusion | flops 47516160 | bytes 6295552 | tf_op jit(solution)/shard_map/dot_general | solution.py:96
  13.1 32.0 %all-reduce.1 = bf16[8,4096]{1,0:T(8,128)(2,1)S(1)} all-reduce(f32[8,4096]{1,0:T(8,128)} %fusion.41), channel_id=1, replica_groups=mesh['ctx'=4,'tp'=4,'grp'=2] {'tp','grp'}, use_global_device_ids=true, to_apply=%region_4.5 | all-reduce | flops 32768 | bytes 196608 | tf_op jit(solution)/shard_map/psum | solution.py:107
  45.2 0.7 reshape.183
  45.8 3.7 %all-to-all-start = ((bf16[4,2,4096]{2,1,0:T(2,128)(2,1)}), bf16[4,2,4096]{2,1,0:T(2,128)(2,1)S(1)}, u32[]{:S(2)}, u32[]{:S(2)}) async-start(bf16[4,2,4096]{2,1,0:T(2,128)(2,1)} %reshape.183), calls=%async_computation | async-start | bytes 131072 | tf_op jit(solution)/shard_map/all_to_all | solution.py:108
  49.6 0.0 all-gather.2.cloned.1.call-start
  49.6 0.7 all-gather.2.cloned.1.call-update
  50.3 0.0 copy-done.5
  50.3 0.2 fusion.112
  50.6 0.1 reduce.2
  50.7 0.6 slice.10
  51.3 0.0 copy-done.1
  51.3 1.3 %gather_fusion = s32[128]{0:T(128)S(1)} fusion(s32[512]{0:T(512)S(1)} %copy-done.1, s32[1024]{0:T(1024)S(1)} %pad_clamp_fusion.1), kind=kCustom, calls=%fused_computation | custom fusion | bytes 1536 | tf_op jit(solution)/shard_map/gather | solution.py:121
  52.6 3.5 %gather_fusion.1 = s32[512]{0:T(512)S(1)} fusion(s32[512]{0:T(512)S(1)} %copy-done.1, s32[1024]{0:T(1024)S(1)} %pad_clamp_fusion), kind=kCustom, calls=%fused_computation.1 | custom fusion | bytes 6144 | tf_op jit(solution)/shard_map/gather | solution.py:39
  56.1 0.1 convert_reduce_fusion
  56.2 0.1 select_reduce_fusion.1
  56.3 0.7 fusion.80
  57.0 0.1 select_reduce_fusion
  57.1 0.8 fusion.19
  57.9 0.7 iota_compare_fusion.4
  58.7 0.0 all-to-all-done
  58.7 2.2 %gather_fusion.2 = bf16[128,4096]{1,0:T(8,128)(2,1)} fusion(bf16[8,4096]{1,0:T(8,128)(2,1)S(1)} %reshape.184, s32[1024]{0:T(1024)S(1)} %pad_clamp_fusion.2), kind=kCustom, calls=%fused_computation.2 | custom fusion | bytes 2097664 | tf_op jit(solution)/shard_map/gather | solution.py:113
  60.9 0.0 copy-start.6
  60.9 12.1 %all-gather.2.cloned.1.call-done = bf16[128,4096]{1,0:T(8,128)(2,1)} async-done(((bf16[128,512]{1,0:T(8,128)(2,1)}), bf16[128,4096]{1,0:T(8,128)(2,1)}) %all-gather.2.cloned.1.call-update) | async-done | bytes 1048592 | tf_op jit(solution)/shard_map/all_gather | solution.py:112
  73.0 2.2 %fusion = (f32[128]{0:T(128)S(1)}, bf16[128,4096]{1,0:T(8,128)(2,1)S(1)}) fusion(bf16[128,4096]{1,0:T(8,128)(2,1)} %gather_fusion.2, bf16[128,4096]{1,0:T(8,128)(2,1)} %all-gather.2.cloned.1.call-done, pred[128]{0:T(512)(128)(4,1)S(1)} %iota_compare_fusion.4), kind=kLoop, calls=%fused_computation.5 | loop fusion | flops 2097024 | bytes 3146368 | tf_op jit(solution)/shard_map/reduce_sum | solution.py:14
  75.2 0.0 copy-start.2
  75.2 0.0 copy-start.7
  75.2 0.0 copy-done.6
  75.2 3.3 %fusion.16 = bf16[128,512]{1,0:T(8,128)(2,1)S(1)} fusion(bf16[4096,512]{1,0:T(8,128)(2,1)} %param.19, bf16[128,4096]{1,0:T(8,128)(2,1)S(1)} %get-tuple-element.6, f32[4096]{0:T(1024)S(1)} %copy-done.6, f32[128]{0:T(128)S(1)} %add_rsqrt_fusion.1), kind=kOutput, calls=%fused_computation.24 | convolution fusion | flops 538968064 | bytes 5390848 | tf_op jit(solution)/shard_map/dot_general | solution.py:116
  78.6 0.0 copy-done.2
  78.6 0.0 copy-done.7
  78.6 9.6 %all_gather.7 = bf16[512,256]{1,0:T(8,128)(2,1)} all-gather(bf16[128,256]{1,0:T(8,128)(2,1)S(1)} %dynamic-slice_convert_fusion), channel_id=1, replica_groups=mesh['ctx'=4,'tp'=4,'grp'=2] {'ctx'}, dimensions={0}, use_global_device_ids=true | all-gather | bytes 327680 | tf_op jit(solution)/shard_map/all_gather | solution.py:126
  88.2 1.0 reshape.185
  89.2 1.1 %fusion.113 = (bf16[512,1,1,128]{3,2,0,1:T(2,128)(2,1)}, bf16[512,1,1,128]{3,2,0,1:T(2,128)(2,1)S(1)}) fusion(bf16[512,1,2,128]{3,2,0,1:T(2,128)(2,1)S(1)} %reshape.185), kind=kLoop, calls=%fused_computation.155 | loop fusion | bytes 524288 | tf_op jit(solution)/shard_map/slice | solution.py:34
  90.3 0.0 copy-start.4
  90.3 0.0 copy-start.3
  90.3 3.3 %fusion.7 = bf16[16,4,8,128]{3,2,1,0:T(8,128)(2,1)S(1)} fusion(bf16[4096,512]{1,0:T(8,128)(2,1)} %param.18, bf16[128,4096]{1,0:T(8,128)(2,1)} %copy-done.2, f32[4096]{0:T(1024)S(1)} %copy-done.6, f32[128]{0:T(128)} %copy-done.7), kind=kOutput, calls=%fused_computation.15 | convolution fusion | flops 539033600 | bytes 5390848 | tf_op jit(solution)/shard_map/dot_general | solution.py:115
  93.6 0.0 copy-done.4
  93.6 1.3 %fusion.114 = (f32[4,128]{1,0:T(4,128)S(1)}, f32[1,4,128,512]{2,3,1,0:T(8,128)}) fusion(bf16[16,4,8,128]{3,2,1,0:T(8,128)(2,1)S(1)} %fusion.7, bf16[512,1,1,128]{3,2,0,1:T(2,128)(2,1)S(1)} %get-tuple-element.10, pred[128,512]{0,1:T(8,128)(4,1)S(1)} %copy-done.4), kind=kOutput, calls=%fused_computation.156 | convolution fusion | flops 67894784 | bytes 1378304 | tf_op jit(solution)/shard_map/qkgd,rkd->kgqr/dot_general | solution.py:45
  94.9 0.0 copy-done.3
  94.9 0.8 copy.27
  95.7 1.4 %fusion.8 = f32[4,128]{1,0:T(4,128)S(1)} fusion(f32[1,4,128,512]{2,3,1,0:T(8,128)} %get-tuple-element.12, f32[4,128]{1,0:T(4,128)S(1)} %broadcast_maximum_fusion, pred[128,512]{0,1:T(8,128)(4,1)} %fusion.19), kind=kLoop, calls=%fused_computation.18 | loop fusion | flops 785920 | bytes 1118208 | tf_op jit(solution)/shard_map/reduce_sum | solution.py:51
  97.1 1.6 %fusion.6 = bf16[128,4,128]{0,2,1:T(8,128)(2,1)S(1)} fusion(f32[1,4,128,512]{2,3,1,0:T(8,128)} %get-tuple-element.12, f32[4,128]{1,0:T(4,128)S(1)} %broadcast_maximum_fusion, pred[128,512]{0,1:T(8,128)(4,1)} %fusion.19, bf16[512,1,1,128]{0,3,2,1:T(8,128)(2,1)} %copy.27, f32[128,4]{0,1:T(4,128)S(1)} %bitcast.62), kind=kOutput, calls=%fused_computation.13 | convolution fusion | flops 68026368 | bytes 1380352 | tf_op jit(solution)/shard_map/kgqr,rkd->kgqd/dot_general | solution.py:52
  98.7 0.8 copy.25
  (18 shorter events, 0.2 us)
Async XLA Ops:
  6.5 2.0 %copy-start = (bf16[5120,320]{0,1:T(8,128)(2,1)S(1)}, bf16[5120,320]{0,1:T(8,128)(2,1)}, u32[]{:S(2)}) copy-start(bf16[5120,320]{0,1:T(8,128)(2,1)} %param.15) | copy-start | bytes 9830404
  8.5 41.8 %copy-start.5 = (s32[4,4]{1,0:T(4,128)S(1)}, s32[4,4]{1,0:T(4,128)}, u32[]{:S(2)}) copy-start(s32[4,4]{1,0:T(4,128)} %param.11) | copy-start | bytes 196
  8.5 42.8 %copy-start.1 = (s32[512]{0:T(512)S(1)}, s32[512]{0:T(512)}, u32[]{:S(2)}) copy-start(s32[512]{0:T(512)} %param.13) | copy-start | bytes 6148
  45.8 12.8 %all-to-all-start = ((bf16[4,2,4096]{2,1,0:T(2,128)(2,1)}), bf16[4,2,4096]{2,1,0:T(2,128)(2,1)S(1)}, u32[]{:S(2)}, u32[]{:S(2)}) async-start(bf16[4,2,4096]{2,1,0:T(2,128)(2,1)} %reshape.183), calls=%async_computation | async-start | bytes 131072 | tf_op jit(solution)/shard_map/all_to_all | solution.py:108
  49.6 23.5 %all-gather.2.cloned.1.call-start = ((), (), s32[]{:S(2)}) async-start(), calls=%async_computation.1 | async-start | bytes 1179648 | tf_op jit(solution)/shard_map/all_gather | solution.py:112
  60.9 14.3 %copy-start.6 = (f32[4096]{0:T(1024)S(1)}, f32[4096]{0:T(1024)}, u32[]{:S(2)}) copy-start(f32[4096]{0:T(1024)} %param.17) | copy-start | bytes 49156
  75.2 3.4 %copy-start.2 = (bf16[128,4096]{1,0:T(8,128)(2,1)}, bf16[128,4096]{1,0:T(8,128)(2,1)S(1)}, u32[]{:S(2)}) copy-start(bf16[128,4096]{1,0:T(8,128)(2,1)S(1)} %get-tuple-element.6) | copy-start | bytes 3145732
  75.2 3.4 %copy-start.7 = (f32[128]{0:T(128)}, f32[128]{0:T(128)S(1)}, u32[]{:S(2)}) copy-start(f32[128]{0:T(128)S(1)} %add_rsqrt_fusion.1) | copy-start | bytes 1540
  90.3 3.3 %copy-start.4 = (pred[128,512]{0,1:T(8,128)(4,1)S(1)}, pred[128,512]{0,1:T(8,128)(4,1)}, u32[]{:S(2)}) copy-start(pred[128,512]{0,1:T(8,128)(4,1)} %fusion.19) | copy-start | bytes 196612
  90.3 4.6 %copy-start.3 = (bf16[512,1,1,128]{3,2,0,1:T(2,128)(2,1)S(1)}, bf16[512,1,1,128]{3,2,0,1:T(2,128)(2,1)}, u32[]{:S(2)}) copy-start(bf16[512,1,1,128]{3,2,0,1:T(2,128)(2,1)} %get-tuple-element.9) | copy-start | bytes 393220
Sparse Core Ops, SparseCore 0:
  52.0 21.0 all-gather.1
where the time goes:
time: 107 us; the launch traced here: 106 us
  blocking collectives  41.6 us (39%)
  matrix products  14.1 us (13%)
  between operations  13.7 us (13%)
  local copies, waits for them, and re-layouts  13 us (12%)
  waiting for transfers between devices  12.8 us (12%)
  other arithmetic  7.46 us (7%)
  starting transfers between devices  3.72 us (3%)
    psum x1, blocking collectives, shards(): merged = lax.psum(partial_value, ('tp', 'grp')).astype(jnp.bfloat16)  32 us
    all_gather x1, waiting for transfers between devices, shards(): text_full = lax.all_gather(text_states, ('tp', 'grp'), axis=1, tiled=True)  12.1 us
    all_gather x1, blocking collectives, shards(): shard_piece = lax.all_gather(chosen, 'ctx', axis=0, tiled=True)  9.55 us
    dot_general x1, matrix products, shards(): jnp.dot(hidden, merge_down, preferred_element_type=jnp.float32)  4.57 us
    all_to_all x1, starting transfers between devices, shards(): lax.all_to_all(merged.reshape(ctx_size, bucket_rows, -1), 'ctx', split_ax...  3.72 us
    gather x1, local copies, waits for them, and re-layouts, attend(): key_seg = segment_ids[key_pos]  3.49 us
    dot_general x1, matrix products, shards(): jnp.dot(normal, kv_weight, preferred_element_type=jnp.float32)  3.34 us
    dot_general x1, matrix products, shards(): jnp.dot(normal, query_weight, preferred_element_type=jnp.float32)  3.32 us
  transfers between devices with their start and end apart: 2, of which 1 were waited for; matrix products, arithmetic and copies ran while one was open for 10% of the time, Pallas kernels for 0%

commit v1 on v0

--- a/solution.py
+++ b/solution.py
@@ -104,7 +104,7 @@
     first_slot = jnp.sum(jnp.where(source_match, count_starts[None, :], 0), axis=1)
     visual = slot_ids < count_ends[ctx_size - 1]
     pick_rows = jnp.where(visual, source * bucket_rows + slot_ids - first_slot, 0)
-    merged = lax.psum(partial_value, ("tp", "grp")).astype(jnp.bfloat16)
+    merged = jnp.sum(lax.all_gather(partial_value, ("tp", "grp")), axis=0).astype(jnp.bfloat16)
     arrived = lax.all_to_all(
         merged.reshape(ctx_size, bucket_rows, -1), "ctx", split_axis=0, concat_axis=0, tiled=True
     )

time: 107 us -> 95.6 us (0.89)
  blocking collectives: 41.6 us -> 9.63 us
  waiting for transfers between devices: 12.8 us -> 32.5 us
  other arithmetic: 7.46 us -> 8.6 us
    psum x1 -> x0, blocking collectives: 32 us -> none  [shards(): merged = lax.psum(partial_value, ('tp', 'grp')).astype(jnp.bfloat16)]
    all_gather x0 -> x1, waiting for transfers between devices: none -> 16.8 us  [shards(): lax.all_gather(partial_value, ('tp', 'grp'))]
    all_to_all x1, waiting for transfers between devices: 0.01 us -> 4.19 us  [shards(): lax.all_to_all(merged.reshape(ctx_size, bucket_rows, -1), 'ctx', split_ax...]
    all_gather x1, waiting for transfers between devices: 12.1 us -> 10.8 us  [shards(): text_full = lax.all_gather(text_states, ('tp', 'grp'), axis=1, tiled=True)]
    reduce_sum x0 -> x1, other arithmetic: none -> 1.28 us  [shards(): jnp.sum(lax.all_gather(partial_value, ('tp', 'grp')), axis=0)]
  transfers between devices with their start and end apart: 2 -> 3, of which waited for: 1 -> 3; matrix products, arithmetic and copies ran while one was open for 10% -> 13% of each run, Pallas kernels for 0% -> 0%
where the time goes in v1:
time: 95.6 us; the launch traced here: 95.1 us
  waiting for transfers between devices  32.5 us (34%)
  matrix products  14.1 us (15%)
  between operations  13.7 us (14%)
  local copies, waits for them, and re-layouts  13 us (14%)
  blocking collectives  9.63 us (10%)
  other arithmetic  8.6 us (9%)
  starting transfers between devices  3.7 us (4%)
    all_gather x1, waiting for transfers between devices, shards(): lax.all_gather(partial_value, ('tp', 'grp'))  16.8 us
    all_gather x1, waiting for transfers between devices, shards(): text_full = lax.all_gather(text_states, ('tp', 'grp'), axis=1, tiled=True)  10.8 us
    all_gather x1, blocking collectives, shards(): shard_piece = lax.all_gather(chosen, 'ctx', axis=0, tiled=True)  9.63 us
    dot_general x1, matrix products, shards(): jnp.dot(hidden, merge_down, preferred_element_type=jnp.float32)  4.57 us
    all_to_all x1, waiting for transfers between devices, shards(): lax.all_to_all(merged.reshape(ctx_size, bucket_rows, -1), 'ctx', split_ax...  4.19 us
    all_to_all x1, starting transfers between devices, shards(): lax.all_to_all(merged.reshape(ctx_size, bucket_rows, -1), 'ctx', split_ax...  3.66 us
    gather x1, local copies, waits for them, and re-layouts, attend(): key_seg = segment_ids[key_pos]  3.49 us
    dot_general x1, matrix products, shards(): jnp.dot(normal, kv_weight, preferred_element_type=jnp.float32)  3.35 us
  transfers between devices with their start and end apart: 3, of which 3 were waited for; matrix products, arithmetic and copies ran while one was open for 13% of the time, Pallas kernels for 0%

profile of v1, /device:TPU:0, one launch (start us, length us, event | category | flops | bytes accessed | tf_op | source)
XLA Modules:
  0.0 95.1 jit_solution(283522146798433267)
XLA Ops:
  6.5 0.0 copy-start
  6.5 0.0 all-gather.6.cloned.1.call-start
  6.5 1.0 %convert_multiply_fusion.3 = f32[8,5120]{1,0:T(8,128)S(1)} fusion(bf16[8,5120]{1,0:T(8,128)(2,1)} %param.10), kind=kLoop, calls=%fused_computation.30 | loop fusion | flops 81920 | bytes 245760 | tf_op jit(solution)/shard_map/mul | solution.py:14
  7.6 0.1 reduce_sum.76
  7.7 0.7 mul.112
  8.4 0.1 mul.109
  8.5 0.0 copy-done
  8.5 0.0 copy-start.5
  8.5 0.0 copy-start.1
  8.5 4.6 %fusion.41 = f32[8,4096]{1,0:T(8,128)} fusion(bf16[320,4096]{1,0:T(8,128)(2,1)} %param.16, bf16[5120,320]{0,1:T(8,128)(2,1)S(1)} %copy-done, f32[8,5120]{1,0:T(8,128)S(1)} %bitcast.61, bf16[8,5120]{1,0:T(8,128)(2,1)} %param.10, f32[5120]{0:T(1024)S(1)} %mul.113), kind=kOutput, calls=%fused_computation.59 | convolution fusion | flops 47516160 | bytes 6295552 | tf_op jit(solution)/shard_map/dot_general | solution.py:96
  13.1 0.0 all-gather.6.cloned.1.call-update
  13.1 0.0 all-gather.4.cloned.1.call-start
  13.2 0.7 all-gather.4.cloned.1.call-update
  13.9 0.0 copy-done.5
  13.9 0.2 fusion.112
  14.1 0.1 reduce.2
  14.2 0.6 slice.10
  14.9 0.0 copy-done.1
  14.9 1.3 %gather_fusion = s32[128]{0:T(128)S(1)} fusion(s32[512]{0:T(512)S(1)} %copy-done.1, s32[1024]{0:T(1024)S(1)} %pad_clamp_fusion.1), kind=kCustom, calls=%fused_computation | custom fusion | bytes 1536 | tf_op jit(solution)/shard_map/gather | solution.py:121
  16.2 3.5 %gather_fusion.1 = s32[512]{0:T(512)S(1)} fusion(s32[512]{0:T(512)S(1)} %copy-done.1, s32[1024]{0:T(1024)S(1)} %pad_clamp_fusion), kind=kCustom, calls=%fused_computation.1 | custom fusion | bytes 6144 | tf_op jit(solution)/shard_map/gather | solution.py:39
  19.7 0.1 convert_reduce_fusion
  19.8 0.1 select_reduce_fusion.1
  19.9 0.6 fusion.80
  20.5 0.1 select_reduce_fusion
  20.6 0.8 fusion.19
  21.4 16.8 %all-gather.6.cloned.1.call-done = f32[64,4096]{1,0:T(8,128)} async-done(((f32[8,4096]{1,0:T(8,128)}), f32[64,4096]{1,0:T(8,128)}) %all-gather.6.cloned.1.call-update) | async-done | bytes 1048592 | tf_op jit(solution)/shard_map/all_gather | solution.py:107
  38.2 1.3 %bitcast_reduce_fusion = bf16[8,4096]{1,0:T(8,128)(2,1)S(1)} fusion(f32[64,4096]{1,0:T(8,128)} %all-gather.6.cloned.1.call-done), kind=kLoop, calls=%fused_computation.16 | loop fusion | flops 229376 | bytes 1114112 | tf_op jit(solution)/shard_map/reduce_sum | solution.py:107
  39.5 0.7 convert_element_type.44
  40.2 3.7 %all-to-all-start = ((bf16[4,2,4096]{2,1,0:T(2,128)(2,1)}), bf16[4,2,4096]{2,1,0:T(2,128)(2,1)S(1)}, u32[]{:S(2)}, u32[]{:S(2)}) async-start(bf16[4,2,4096]{2,1,0:T(2,128)(2,1)} %convert_element_type.44), calls=%async_computation | async-start | bytes 131072 | tf_op jit(solution)/shard_map/all_to_all | solution.py:108
  43.9 0.6 iota_compare_fusion.4
  44.5 4.2 %all-to-all-done = bf16[4,2,4096]{2,1,0:T(2,128)(2,1)S(1)} async-done(((bf16[4,2,4096]{2,1,0:T(2,128)(2,1)}), bf16[4,2,4096]{2,1,0:T(2,128)(2,1)S(1)}, u32[]{:S(2)}, u32[]{:S(2)}) %all-to-all-start) | async-done | bytes 65568 | tf_op jit(solution)/shard_map/all_to_all | solution.py:108
  48.8 2.2 %gather_fusion.2 = bf16[128,4096]{1,0:T(8,128)(2,1)} fusion(bf16[8,4096]{1,0:T(8,128)(2,1)S(1)} %reshape.183, s32[1024]{0:T(1024)S(1)} %pad_clamp_fusion.2), kind=kCustom, calls=%fused_computation.2 | custom fusion | bytes 2097664 | tf_op jit(solution)/shard_map/gather | solution.py:113
  51.0 0.0 copy-start.6
  51.0 10.8 %all-gather.4.cloned.1.call-done = bf16[128,4096]{1,0:T(8,128)(2,1)} async-done(((bf16[128,512]{1,0:T(8,128)(2,1)}), bf16[128,4096]{1,0:T(8,128)(2,1)}) %all-gather.4.cloned.1.call-update) | async-done | bytes 1048592 | tf_op jit(solution)/shard_map/all_gather | solution.py:112
  61.7 2.2 %fusion = (f32[128]{0:T(128)S(1)}, bf16[128,4096]{1,0:T(8,128)(2,1)S(1)}) fusion(bf16[128,4096]{1,0:T(8,128)(2,1)} %gather_fusion.2, bf16[128,4096]{1,0:T(8,128)(2,1)} %all-gather.4.cloned.1.call-done, pred[128]{0:T(512)(128)(4,1)S(1)} %iota_compare_fusion.4), kind=kLoop, calls=%fused_computation.5 | loop fusion | flops 2097024 | bytes 3146368 | tf_op jit(solution)/shard_map/reduce_sum | solution.py:14
  63.9 0.0 copy-start.2
  63.9 0.0 copy-start.7
  63.9 0.0 copy-done.6
  63.9 3.3 %fusion.16 = bf16[128,512]{1,0:T(8,128)(2,1)S(1)} fusion(bf16[4096,512]{1,0:T(8,128)(2,1)} %param.19, bf16[128,4096]{1,0:T(8,128)(2,1)S(1)} %get-tuple-element.6, f32[4096]{0:T(1024)S(1)} %copy-done.6, f32[128]{0:T(128)S(1)} %add_rsqrt_fusion.1), kind=kOutput, calls=%fused_computation.25 | convolution fusion | flops 538968064 | bytes 5390848 | tf_op jit(solution)/shard_map/dot_general | solution.py:116
  67.3 0.0 copy-done.2
  67.3 0.0 copy-done.7
  67.3 9.6 %all_gather.15 = bf16[512,256]{1,0:T(8,128)(2,1)} all-gather(bf16[128,256]{1,0:T(8,128)(2,1)S(1)} %dynamic-slice_convert_fusion), channel_id=1, replica_groups=mesh['ctx'=4,'tp'=4,'grp'=2] {'ctx'}, dimensions={0}, use_global_device_ids=true | all-gather | bytes 327680 | tf_op jit(solution)/shard_map/all_gather | solution.py:126
  77.0 1.0 %reshape.184 = bf16[512,1,2,128]{3,2,0,1:T(2,128)(2,1)S(1)} reshape(bf16[512,256]{1,0:T(8,128)(2,1)} %all_gather.15) | data formatting | bytes 524288 | tf_op jit(solution)/shard_map/reshape | solution.py:32
  78.0 1.1 %fusion.113 = (bf16[512,1,1,128]{3,2,0,1:T(2,128)(2,1)}, bf16[512,1,1,128]{3,2,0,1:T(2,128)(2,1)S(1)}) fusion(bf16[512,1,2,128]{3,2,0,1:T(2,128)(2,1)S(1)} %reshape.184), kind=kLoop, calls=%fused_computation.156 | loop fusion | bytes 524288 | tf_op jit(solution)/shard_map/slice | solution.py:34
  79.1 0.0 copy-start.4
  79.1 0.0 copy-start.3
  79.1 3.3 %fusion.7 = bf16[16,4,8,128]{3,2,1,0:T(8,128)(2,1)S(1)} fusion(bf16[4096,512]{1,0:T(8,128)(2,1)} %param.18, bf16[128,4096]{1,0:T(8,128)(2,1)} %copy-done.2, f32[4096]{0:T(1024)S(1)} %copy-done.6, f32[128]{0:T(128)} %copy-done.7), kind=kOutput, calls=%fused_computation.15 | convolution fusion | flops 539033600 | bytes 5390848 | tf_op jit(solution)/shard_map/dot_general | solution.py:115
  82.4 0.0 copy-done.4
  82.4 1.3 %fusion.114 = (f32[4,128]{1,0:T(4,128)S(1)}, f32[1,4,128,512]{2,3,1,0:T(8,128)}) fusion(bf16[16,4,8,128]{3,2,1,0:T(8,128)(2,1)S(1)} %fusion.7, bf16[512,1,1,128]{3,2,0,1:T(2,128)(2,1)S(1)} %get-tuple-element.10, pred[128,512]{0,1:T(8,128)(4,1)S(1)} %copy-done.4), kind=kOutput, calls=%fused_computation.157 | convolution fusion | flops 67894784 | bytes 1378304 | tf_op jit(solution)/shard_map/qkgd,rkd->kgqr/dot_general | solution.py:45
  83.7 0.0 copy-done.3
  83.7 0.8 copy.27
  84.5 1.4 %fusion.8 = f32[4,128]{1,0:T(4,128)S(1)} fusion(f32[1,4,128,512]{2,3,1,0:T(8,128)} %get-tuple-element.12, f32[4,128]{1,0:T(4,128)S(1)} %broadcast_maximum_fusion, pred[128,512]{0,1:T(8,128)(4,1)} %fusion.19), kind=kLoop, calls=%fused_computation.19 | loop fusion | flops 785920 | bytes 1118208 | tf_op jit(solution)/shard_map/reduce_sum | solution.py:51
  85.9 1.6 %fusion.6 = bf16[128,4,128]{0,2,1:T(8,128)(2,1)S(1)} fusion(f32[1,4,128,512]{2,3,1,0:T(8,128)} %get-tuple-element.12, f32[4,128]{1,0:T(4,128)S(1)} %broadcast_maximum_fusion, pred[128,512]{0,1:T(8,128)(4,1)} %fusion.19, bf16[512,1,1,128]{0,3,2,1:T(8,128)(2,1)} %copy.27, f32[128,4]{0,1:T(4,128)S(1)} %bitcast.64), kind=kOutput, calls=%fused_computation.13 | convolution fusion | flops 68026368 | bytes 1380352 | tf_op jit(solution)/shard_map/kgqr,rkd->kgqd/dot_general | solution.py:52
  87.5 0.8 copy.25
  (18 shorter events, 0.2 us)
Async XLA Ops:
  6.5 2.0 %copy-start = (bf16[5120,320]{0,1:T(8,128)(2,1)S(1)}, bf16[5120,320]{0,1:T(8,128)(2,1)}, u32[]{:S(2)}) copy-start(bf16[5120,320]{0,1:T(8,128)(2,1)} %param.15) | copy-start | bytes 9830404
  6.5 31.7 %all-gather.6.cloned.1.call-start = ((), (), s32[]{:S(2)}) async-start(), calls=%async_computation.2 | async-start | bytes 1179648 | tf_op jit(solution)/shard_map/all_gather | solution.py:107
  8.5 5.4 %copy-start.5 = (s32[4,4]{1,0:T(4,128)S(1)}, s32[4,4]{1,0:T(4,128)}, u32[]{:S(2)}) copy-start(s32[4,4]{1,0:T(4,128)} %param.11) | copy-start | bytes 196
  8.5 6.4 %copy-start.1 = (s32[512]{0:T(512)S(1)}, s32[512]{0:T(512)}, u32[]{:S(2)}) copy-start(s32[512]{0:T(512)} %param.13) | copy-start | bytes 6148
  13.1 48.6 %all-gather.4.cloned.1.call-start = ((), (), s32[]{:S(2)}) async-start(), calls=%async_computation.1 | async-start | bytes 1179648 | tf_op jit(solution)/shard_map/all_gather | solution.py:112
  40.2 8.5 %all-to-all-start = ((bf16[4,2,4096]{2,1,0:T(2,128)(2,1)}), bf16[4,2,4096]{2,1,0:T(2,128)(2,1)S(1)}, u32[]{:S(2)}, u32[]{:S(2)}) async-start(bf16[4,2,4096]{2,1,0:T(2,128)(2,1)} %convert_element_type.44), calls=%async_computation | async-start | bytes 131072 | tf_op jit(solution)/shard_map/all_to_all | solution.py:108
  51.0 13.0 %copy-start.6 = (f32[4096]{0:T(1024)S(1)}, f32[4096]{0:T(1024)}, u32[]{:S(2)}) copy-start(f32[4096]{0:T(1024)} %param.17) | copy-start | bytes 49156
  63.9 3.4 %copy-start.2 = (bf16[128,4096]{1,0:T(8,128)(2,1)}, bf16[128,4096]{1,0:T(8,128)(2,1)S(1)}, u32[]{:S(2)}) copy-start(bf16[128,4096]{1,0:T(8,128)(2,1)S(1)} %get-tuple-element.6) | copy-start | bytes 3145732
  63.9 3.4 %copy-start.7 = (f32[128]{0:T(128)}, f32[128]{0:T(128)S(1)}, u32[]{:S(2)}) copy-start(f32[128]{0:T(128)S(1)} %add_rsqrt_fusion.1) | copy-start | bytes 1540
  79.1 3.3 %copy-start.4 = (pred[128,512]{0,1:T(8,128)(4,1)S(1)}, pred[128,512]{0,1:T(8,128)(4,1)}, u32[]{:S(2)}) copy-start(pred[128,512]{0,1:T(8,128)(4,1)} %fusion.19) | copy-start | bytes 196612
  79.1 4.6 %copy-start.3 = (bf16[512,1,1,128]{3,2,0,1:T(2,128)(2,1)S(1)}, bf16[512,1,1,128]{3,2,0,1:T(2,128)(2,1)}, u32[]{:S(2)}) copy-start(bf16[512,1,1,128]{3,2,0,1:T(2,128)(2,1)} %get-tuple-element.9) | copy-start | bytes 393220
Sparse Core Ops, SparseCore 0:
  13.3 24.9 all-gather.5
  39.9 21.8 all-gather.3
